TPU v7x, 512 devices: a whole 4x4x16 slice. The times are simulated.
512 devices in a mesh: fsdp: 16 (over x, y), dp: 32 (over z, core).
Axes of the slice: x: 4, y: 4, z: 16, core: 2. Of those that a mesh axis runs over, the one named last changes fastest.
Arguments:
- tokens: bfloat16 [65536, 4096], P(('fsdp', 'dp')), may hold values from -6 to 6
- master_old: float32 [512, 128, 128], P(('fsdp', 'dp')), may hold values from -0.25 to 0.25
- moment_old: float32 [512, 128, 128], P(('fsdp', 'dp')), may hold values from -6 to 6
- second_old: float32 [512, 128, 128], P(('fsdp', 'dp')), may hold values from 0.01 to 1
- old_cell: int32 [112, 4], P('fsdp'), may hold values from 0 to 31, as said below
- new_cell: int32 [112, 4], P('fsdp'), may hold values from 0 to 31, as said below
- regrown: int32 [112, 4], P('fsdp'), may hold values 0 or 1
- new_rows: int32 [112, 4], replicated, may hold values from 0 to 31, as said below
Outputs:
- hidden: bfloat16 [65536, 14336], P(('fsdp', 'dp'))
- master_new: float32 [512, 128, 128], P(('fsdp', 'dp'))
- moment_new: float32 [512, 128, 128], P(('fsdp', 'dp'))
- second_new: float32 [512, 128, 128], P(('fsdp', 'dp'))
Inputs may be any that keep to these rules, and one draw needn't show every extreme that they name: `old_cell`: within one fsdp index, taking its slots column by column and then by k, the old cells strictly increase; a cell's index // 1 is its holder along dp and index % 1 its place in that holder's buffer. `new_cell`: strictly increasing in the same order; every slot's new cell differs from its old cell by at most 4, and by exactly 4 for some slot of every fsdp index. `new_rows`: the 4 block rows of one block column are distinct.
All inputs are finite; a program needn't handle non-finite values. No bound on the sum of `regrown` on one device may be relied on, other than what follows from the above.
Results may differ from a plain program's by a relative error of at most 0.007.
Values may be sent and summed in bfloat16 or wider, within the bound.
No kernel may reach another device: no remote copies, remote signals or barrier semaphores. Data moves between devices by JAX's collectives and lax.ppermute only.
A program may use at most 128 MiB of HBM per device.

v0:
```python
import jax
import jax.numpy as jnp
from jax import lax
from jax.sharding import PartitionSpec as P


def passed_along(block, axis, distance):
    devices = range(lax.axis_size(axis))
    route = [(i - distance, i) for i in devices if i - distance in devices]
    return lax.ppermute(block, axis, route)


def on_device(tokens, master_old, moment_old, second_old, old_cell, new_cell, regrown, new_rows):
    block_size = master_old.shape[1]
    capacity = master_old.shape[0]
    column_count = old_cell.shape[0]
    nonzero_count = old_cell.shape[1]
    slot_count = column_count * nonzero_count
    axis_width = lax.axis_size("dp")
    cell_count = axis_width * capacity
    farthest = min((cell_count - slot_count + capacity - 1) // capacity, axis_width - 1)
    holder = lax.axis_index("dp")
    old_flat = old_cell.reshape(-1)
    new_flat = new_cell.reshape(-1)
    keep_flag = regrown.reshape(-1) == 0
    my_cells = holder * capacity + jnp.arange(capacity, dtype=jnp.int32)
    matches = new_flat[None, :] == my_cells[:, None]
    present = jnp.any(matches & keep_flag[None, :], axis=1)
    source = jnp.sum(jnp.where(matches, old_flat[None, :], 0), axis=1)
    offset = holder - source // capacity
    slot_place = source % capacity
    candidate = jnp.where(offset > 0, 2 * offset - 1, jnp.where(offset < 0, -2 * offset, 0))
    pick_index = candidate * capacity + slot_place
    own_states = (master_old, moment_old, second_old)
    shift_list = []
    for distance in range(1, farthest + 1):
        shift_list.append(distance)
        shift_list.append(-distance)
    received_list = [own_states]
    for by_value in shift_list:
        received_list.append(
            (
                passed_along(own_states[0].astype(jnp.bfloat16), "dp", by_value).astype(
                    jnp.float32
                ),
                passed_along(own_states[1].astype(jnp.bfloat16), "dp", by_value).astype(
                    jnp.float32
                ),
                passed_along(own_states[2].astype(jnp.bfloat16), "dp", by_value).astype(
                    jnp.float32
                ),
            )
        )

    def settle(member):
        pool = jnp.concatenate([entry[member] for entry in received_list], axis=0)
        chosen = jnp.take(pool, pick_index, axis=0, mode="clip")
        return jnp.where(present[:, None, None], chosen, jnp.float32(0.0))

    master_new = settle(0)
    moment_new = settle(1)
    second_new = settle(2)
    cell_blocks = master_new.astype(jnp.bfloat16)
    group_cells = lax.all_gather(cell_blocks, "dp", axis=0, tiled=True)
    panel = jnp.take(group_cells, new_flat, axis=0).reshape(
        column_count, nonzero_count, block_size, block_size
    )
    token_count = tokens.shape[0]
    token_blocks = tokens.reshape(token_count, tokens.shape[1] // block_size, block_size)
    panel_piece = lax.all_gather(panel, "fsdp", axis=0, tiled=True)
    count = panel_piece.shape[0]
    picked = jnp.take(token_blocks, new_rows.reshape(-1), axis=1)
    picked = picked.reshape(token_count, count, nonzero_count, block_size)
    product = jnp.einsum("tcka,ckab->tcb", picked, panel_piece, preferred_element_type=jnp.float32)
    hidden = product.reshape(token_count, count * block_size).astype(jnp.bfloat16)
    return (hidden, master_new, moment_new, second_new)


def solution(mesh):
    return jax.shard_map(
        on_device,
        mesh=mesh,
        in_specs=(
            P(("fsdp", "dp"), None),
            P(("fsdp", "dp"), None, None),
            P(("fsdp", "dp"), None, None),
            P(("fsdp", "dp"), None, None),
            P("fsdp", None),
            P("fsdp", None),
            P("fsdp", None),
            P(),
        ),
        out_specs=(
            P(("fsdp", "dp"), None),
            P(("fsdp", "dp"), None, None),
            P(("fsdp", "dp"), None, None),
            P(("fsdp", "dp"), None, None),
        ),
        check_vma=False,
    )
```

profile of v0, /device:TPU:1, one launch (start us, length us, event | category | flops | bytes accessed | tf_op | source)
XLA Modules:
  0.0 264.1 jit_solution(16962180668199227297)
XLA Ops:
  7.2 0.0 all-gather.3.cloned.1.call-start
  7.2 0.9 fusion.11
  8.1 4.9 %collective-permute-start = (bf16[1,128,128]{2,1,0:T(8,128)(2,1)S(1)}, bf16[1,128,128]{2,1,0:T(8,128)(2,1)S(1)}, u32[]{:S(2)}, u32[]{:S(2)}) collective-permute-start(bf16[1,128,128]{2,1,0:T(8,128)(2,1)S(1)} %get-tuple-element.61), channel_id=1, source_target_pairs={{0,1},{1,2},{2,3},{3,4},{4,5},{5,6},{6,7},{7,8},{8,9},{9,10},{10,1... | collective-permute-start | bytes 98312 | tf_op jit(solution)/shard_map/ppermute | solution.py:10
  13.1 5.1 %collective-permute-start.1 = (bf16[1,128,128]{2,1,0:T(8,128)(2,1)S(1)}, bf16[1,128,128]{2,1,0:T(8,128)(2,1)S(1)}, u32[]{:S(2)}, u32[]{:S(2)}) collective-permute-start(bf16[1,128,128]{2,1,0:T(8,128)(2,1)S(1)} %get-tuple-element.61), channel_id=1, source_target_pairs={{1,0},{2,1},{3,2},{4,3},{5,4},{6,5},{7,6},{8,7},{9,8},{10,9},{11,1... | collective-permute-start | bytes 98312 | tf_op jit(solution)/shard_map/ppermute | solution.py:10
  18.2 1.3 collective-permute-start.2
  19.5 1.3 collective-permute-start.3
  20.8 5.0 %collective-permute-start.4 = (bf16[1,128,128]{2,1,0:T(8,128)(2,1)S(1)}, bf16[1,128,128]{2,1,0:T(8,128)(2,1)S(1)}, u32[]{:S(2)}, u32[]{:S(2)}) collective-permute-start(bf16[1,128,128]{2,1,0:T(8,128)(2,1)S(1)} %get-tuple-element.61), channel_id=1, source_target_pairs={{0,3},{1,4},{2,5},{3,6},{4,7},{5,8},{6,9},{7,10},{8,11},{9,12},{10... | collective-permute-start | bytes 98312 | tf_op jit(solution)/shard_map/ppermute | solution.py:10
  25.9 1.4 and_reduce_fusion
  27.3 1.3 select_reduce_fusion
  29.3 0.0 collective-permute-done
  29.3 1.3 collective-permute-start.5
  30.6 9.2 %collective-permute-start.6 = (bf16[1,128,128]{2,1,0:T(8,128)(2,1)S(1)}, bf16[1,128,128]{2,1,0:T(8,128)(2,1)S(1)}, u32[]{:S(2)}, u32[]{:S(2)}) collective-permute-start(bf16[1,128,128]{2,1,0:T(8,128)(2,1)S(1)} %get-tuple-element.61), channel_id=1, source_target_pairs={{0,4},{1,5},{2,6},{3,7},{4,8},{5,9},{6,10},{7,11},{8,12},{9,13},{1... | collective-permute-start | bytes 98312 | tf_op jit(solution)/shard_map/ppermute | solution.py:10
  39.8 0.0 collective-permute-done.2
  39.8 1.3 collective-permute-start.7
  41.1 0.0 collective-permute-done.5
  41.2 0.0 collective-permute-done.6
  41.2 4.1 %collective-permute-done.7 = bf16[1,128,128]{2,1,0:T(8,128)(2,1)S(1)} collective-permute-done((bf16[1,128,128]{2,1,0:T(8,128)(2,1)S(1)}, bf16[1,128,128]{2,1,0:T(8,128)(2,1)S(1)}, u32[]{:S(2)}, u32[]{:S(2)}) %collective-permute-start.7) | collective-permute-done | bytes 32800 | tf_op jit(solution)/shard_map/ppermute | solution.py:10
  45.3 1.3 fusion.8
  46.6 0.0 all-gather.3.cloned.1.call-update
  46.6 0.0 all-gather.5.cloned.1.call-start
  46.7 0.8 copy.33
  47.5 0.1 reshape.158
  47.5 0.1 copy.32
  47.7 73.8 %all-gather.3.cloned.1.call-done = bf16[32,128,128]{2,1,0:T(8,128)(2,1)} async-done(((bf16[1,128,128]{2,1,0:T(8,128)(2,1)}), bf16[32,128,128]{2,1,0:T(8,128)(2,1)}) %all-gather.3.cloned.1.call-update) | async-done | bytes 1048592 | tf_op jit(solution)/shard_map/all_gather | solution.py:64
  121.4 1.9 gather_fusion
  123.4 1.1 broadcast_select_fusion
  124.4 0.0 all-gather.5.cloned.1.call-update
  124.5 0.9 fusion.9
  125.4 3.2 %collective-permute-start.16 = (bf16[1,128,128]{2,1,0:T(8,128)(2,1)S(1)}, bf16[1,128,128]{2,1,0:T(8,128)(2,1)S(1)}, u32[]{:S(2)}, u32[]{:S(2)}) collective-permute-start(bf16[1,128,128]{2,1,0:T(8,128)(2,1)S(1)} %get-tuple-element.57), channel_id=1, source_target_pairs={{0,1},{1,2},{2,3},{3,4},{4,5},{5,6},{6,7},{7,8},{8,9},{9,10},{10,1... | collective-permute-start | bytes 98312 | tf_op jit(solution)/shard_map/ppermute | solution.py:10
  128.6 1.9 collective-permute-start.17
  130.5 2.3 collective-permute-start.18
  132.8 1.3 collective-permute-start.19
  134.1 6.0 %collective-permute-start.20 = (bf16[1,128,128]{2,1,0:T(8,128)(2,1)S(1)}, bf16[1,128,128]{2,1,0:T(8,128)(2,1)S(1)}, u32[]{:S(2)}, u32[]{:S(2)}) collective-permute-start(bf16[1,128,128]{2,1,0:T(8,128)(2,1)S(1)} %get-tuple-element.57), channel_id=1, source_target_pairs={{0,3},{1,4},{2,5},{3,6},{4,7},{5,8},{6,9},{7,10},{8,11},{9,12},{10... | collective-permute-start | bytes 98312 | tf_op jit(solution)/shard_map/ppermute | solution.py:10
  140.1 0.8 copy.36
  140.9 0.1 reshape.160
  141.0 0.7 compare_and_fusion
  141.7 0.9 fusion.10
  142.7 1.6 copy.35
  144.3 0.7 copy.37
  145.0 0.1 copy.34
  145.1 13.3 %gather_fusion.1 = bf16[448,128,128]{2,1,0:T(8,128)(2,1)} fusion(bf16[128,32,128]{2,0,1:T(8,128)(2,1)S(1)} %copy.37, s32[1024]{0:T(1024)S(1)} %pad_clamp_fusion), kind=kCustom, calls=%fused_computation.1 | custom fusion | bytes 29361920 | tf_op jit(solution)/shard_map/jit(_take)/gather | solution.py:72
  158.3 0.0 collective-permute-done.16
  158.4 1.3 collective-permute-start.21
  159.7 6.6 %collective-permute-start.22 = (bf16[1,128,128]{2,1,0:T(8,128)(2,1)S(1)}, bf16[1,128,128]{2,1,0:T(8,128)(2,1)S(1)}, u32[]{:S(2)}, u32[]{:S(2)}) collective-permute-start(bf16[1,128,128]{2,1,0:T(8,128)(2,1)S(1)} %get-tuple-element.57), channel_id=1, source_target_pairs={{0,4},{1,5},{2,6},{3,7},{4,8},{5,9},{6,10},{7,11},{8,12},{9,13},{1... | collective-permute-start | bytes 98312 | tf_op jit(solution)/shard_map/ppermute | solution.py:10
  166.3 1.3 collective-permute-start.23
  167.6 2.2 collective-permute-start.8
  169.8 0.0 collective-permute-done.20
  169.8 2.2 collective-permute-start.9
  172.0 0.0 collective-permute-done.21
  172.0 6.4 %collective-permute-start.10 = (bf16[1,128,128]{2,1,0:T(8,128)(2,1)S(1)}, bf16[1,128,128]{2,1,0:T(8,128)(2,1)S(1)}, u32[]{:S(2)}, u32[]{:S(2)}) collective-permute-start(bf16[1,128,128]{2,1,0:T(8,128)(2,1)S(1)} %get-tuple-element.59), channel_id=1, source_target_pairs={{0,2},{1,3},{2,4},{3,5},{4,6},{5,7},{6,8},{7,9},{8,10},{9,11},{10,... | collective-permute-start | bytes 98312 | tf_op jit(solution)/shard_map/ppermute | solution.py:10
  178.5 1.3 collective-permute-start.11
  179.8 6.0 %collective-permute-start.12 = (bf16[1,128,128]{2,1,0:T(8,128)(2,1)S(1)}, bf16[1,128,128]{2,1,0:T(8,128)(2,1)S(1)}, u32[]{:S(2)}, u32[]{:S(2)}) collective-permute-start(bf16[1,128,128]{2,1,0:T(8,128)(2,1)S(1)} %get-tuple-element.59), channel_id=1, source_target_pairs={{0,3},{1,4},{2,5},{3,6},{4,7},{5,8},{6,9},{7,10},{8,11},{9,12},{10... | collective-permute-start | bytes 98312 | tf_op jit(solution)/shard_map/ppermute | solution.py:10
  185.9 0.0 collective-permute-done.8
  185.9 1.3 collective-permute-start.13
  187.2 0.0 collective-permute-done.9
  187.2 8.8 %collective-permute-start.14 = (bf16[1,128,128]{2,1,0:T(8,128)(2,1)S(1)}, bf16[1,128,128]{2,1,0:T(8,128)(2,1)S(1)}, u32[]{:S(2)}, u32[]{:S(2)}) collective-permute-start(bf16[1,128,128]{2,1,0:T(8,128)(2,1)S(1)} %get-tuple-element.59), channel_id=1, source_target_pairs={{0,4},{1,5},{2,6},{3,7},{4,8},{5,9},{6,10},{7,11},{8,12},{9,13},{1... | collective-permute-start | bytes 98312 | tf_op jit(solution)/shard_map/ppermute | solution.py:10
  196.0 0.0 collective-permute-done.10
  196.0 1.3 collective-permute-start.15
  197.5 1.3 dynamic-slice_select_fusion
  198.7 3.3 %collective-permute-done.15 = bf16[1,128,128]{2,1,0:T(8,128)(2,1)S(1)} collective-permute-done((bf16[1,128,128]{2,1,0:T(8,128)(2,1)S(1)}, bf16[1,128,128]{2,1,0:T(8,128)(2,1)S(1)}, u32[]{:S(2)}, u32[]{:S(2)}) %collective-permute-start.15) | collective-permute-done | bytes 32800 | tf_op jit(solution)/shard_map/ppermute | solution.py:10
  202.0 1.3 dynamic-slice_select_fusion.1
  203.3 34.5 %all-gather.5.cloned.1.call-done = bf16[112,4,128,128]{3,2,1,0:T(8,128)(2,1)} async-done(((bf16[7,4,128,128]{3,2,1,0:T(8,128)(2,1)}), bf16[112,4,128,128]{3,2,1,0:T(8,128)(2,1)}) %all-gather.5.cloned.1.call-update) | async-done | bytes 14680080 | tf_op jit(solution)/shard_map/all_gather | solution.py:70
  237.7 13.5 %bitcast_convert_fusion = bf16[112,128,128]{2,1,0:T(8,128)(2,1)} fusion(bf16[112,4,128,128]{3,2,1,0:T(8,128)(2,1)} %all-gather.5.cloned.1.call-done, bf16[128,112,4,128]{3,0,2,1:T(8,128)(2,1)} %bitcast.15, pred[112,4]{1,0:T(8,128)(4,1)S(1)} %copy.34), kind=kOutput, calls=%fused_computation.5 | convolution fusion | flops 1888223232 | bytes 33030592 | tf_op jit(solution)/shard_map/tcka,ckab->tcb/dot_general | solution.py:74
  251.2 6.1 %copy.39 = bf16[128,14336]{1,0:T(8,128)(2,1)} copy(bf16[128,14336]{0,1:T(8,128)(2,1)} %bitcast.17) | data formatting | bytes 7340032
  (40 shorter events, 0.2 us)
Async XLA Ops:
  7.2 114.3 %all-gather.3.cloned.1.call-start = ((), (), s32[]{:S(2)}) async-start(), calls=%async_computation | async-start | bytes 1081344 | tf_op jit(solution)/shard_map/all_gather | solution.py:64
  8.1 21.1 %collective-permute-start = (bf16[1,128,128]{2,1,0:T(8,128)(2,1)S(1)}, bf16[1,128,128]{2,1,0:T(8,128)(2,1)S(1)}, u32[]{:S(2)}, u32[]{:S(2)}) collective-permute-start(bf16[1,128,128]{2,1,0:T(8,128)(2,1)S(1)} %get-tuple-element.61), channel_id=1, source_target_pairs={{0,1},{1,2},{2,3},{3,4},{4,5},{5,6},{6,7},{7,8},{8,9},{9,10},{10,1... | collective-permute-start | bytes 98312 | tf_op jit(solution)/shard_map/ppermute | solution.py:10
  13.1 17.5 %collective-permute-start.1 = (bf16[1,128,128]{2,1,0:T(8,128)(2,1)S(1)}, bf16[1,128,128]{2,1,0:T(8,128)(2,1)S(1)}, u32[]{:S(2)}, u32[]{:S(2)}) collective-permute-start(bf16[1,128,128]{2,1,0:T(8,128)(2,1)S(1)} %get-tuple-element.61), channel_id=1, source_target_pairs={{1,0},{2,1},{3,2},{4,3},{5,4},{6,5},{7,6},{8,7},{9,8},{10,9},{11,1... | collective-permute-start | bytes 98312 | tf_op jit(solution)/shard_map/ppermute | solution.py:10
  18.2 21.5 %collective-permute-start.2 = (bf16[1,128,128]{2,1,0:T(8,128)(2,1)S(1)}, bf16[1,128,128]{2,1,0:T(8,128)(2,1)S(1)}, u32[]{:S(2)}, u32[]{:S(2)}) collective-permute-start(bf16[1,128,128]{2,1,0:T(8,128)(2,1)S(1)} %get-tuple-element.61), channel_id=1, source_target_pairs={{0,2},{1,3},{2,4},{3,5},{4,6},{5,7},{6,8},{7,9},{8,10},{9,11},{10,... | collective-permute-start | bytes 98312 | tf_op jit(solution)/shard_map/ppermute | solution.py:10
  19.5 21.6 %collective-permute-start.3 = (bf16[1,128,128]{2,1,0:T(8,128)(2,1)S(1)}, bf16[1,128,128]{2,1,0:T(8,128)(2,1)S(1)}, u32[]{:S(2)}, u32[]{:S(2)}) collective-permute-start(bf16[1,128,128]{2,1,0:T(8,128)(2,1)S(1)} %get-tuple-element.61), channel_id=1, source_target_pairs={{2,0},{3,1},{4,2},{5,3},{6,4},{7,5},{8,6},{9,7},{10,8},{11,9},{12,... | collective-permute-start | bytes 98312 | tf_op jit(solution)/shard_map/ppermute | solution.py:10
  20.8 20.3 %collective-permute-start.4 = (bf16[1,128,128]{2,1,0:T(8,128)(2,1)S(1)}, bf16[1,128,128]{2,1,0:T(8,128)(2,1)S(1)}, u32[]{:S(2)}, u32[]{:S(2)}) collective-permute-start(bf16[1,128,128]{2,1,0:T(8,128)(2,1)S(1)} %get-tuple-element.61), channel_id=1, source_target_pairs={{0,3},{1,4},{2,5},{3,6},{4,7},{5,8},{6,9},{7,10},{8,11},{9,12},{10... | collective-permute-start | bytes 98312 | tf_op jit(solution)/shard_map/ppermute | solution.py:10
  29.3 11.9 %collective-permute-start.5 = (bf16[1,128,128]{2,1,0:T(8,128)(2,1)S(1)}, bf16[1,128,128]{2,1,0:T(8,128)(2,1)S(1)}, u32[]{:S(2)}, u32[]{:S(2)}) collective-permute-start(bf16[1,128,128]{2,1,0:T(8,128)(2,1)S(1)} %get-tuple-element.61), channel_id=1, source_target_pairs={{3,0},{4,1},{5,2},{6,3},{7,4},{8,5},{9,6},{10,7},{11,8},{12,9},{13... | collective-permute-start | bytes 98312 | tf_op jit(solution)/shard_map/ppermute | solution.py:10
  30.6 10.6 %collective-permute-start.6 = (bf16[1,128,128]{2,1,0:T(8,128)(2,1)S(1)}, bf16[1,128,128]{2,1,0:T(8,128)(2,1)S(1)}, u32[]{:S(2)}, u32[]{:S(2)}) collective-permute-start(bf16[1,128,128]{2,1,0:T(8,128)(2,1)S(1)} %get-tuple-element.61), channel_id=1, source_target_pairs={{0,4},{1,5},{2,6},{3,7},{4,8},{5,9},{6,10},{7,11},{8,12},{9,13},{1... | collective-permute-start | bytes 98312 | tf_op jit(solution)/shard_map/ppermute | solution.py:10
  39.8 5.6 %collective-permute-start.7 = (bf16[1,128,128]{2,1,0:T(8,128)(2,1)S(1)}, bf16[1,128,128]{2,1,0:T(8,128)(2,1)S(1)}, u32[]{:S(2)}, u32[]{:S(2)}) collective-permute-start(bf16[1,128,128]{2,1,0:T(8,128)(2,1)S(1)} %get-tuple-element.61), channel_id=1, source_target_pairs={{4,0},{5,1},{6,2},{7,3},{8,4},{9,5},{10,6},{11,7},{12,8},{13,9},{1... | collective-permute-start | bytes 98312 | tf_op jit(solution)/shard_map/ppermute | solution.py:10
  46.6 191.1 %all-gather.5.cloned.1.call-start = ((), (), s32[]{:S(2)}) async-start(), calls=%async_computation.1 | async-start | bytes 15597568 | tf_op jit(solution)/shard_map/all_gather | solution.py:70
  125.4 32.9 %collective-permute-start.16 = (bf16[1,128,128]{2,1,0:T(8,128)(2,1)S(1)}, bf16[1,128,128]{2,1,0:T(8,128)(2,1)S(1)}, u32[]{:S(2)}, u32[]{:S(2)}) collective-permute-start(bf16[1,128,128]{2,1,0:T(8,128)(2,1)S(1)} %get-tuple-element.57), channel_id=1, source_target_pairs={{0,1},{1,2},{2,3},{3,4},{4,5},{5,6},{6,7},{7,8},{8,9},{9,10},{10,1... | collective-permute-start | bytes 98312 | tf_op jit(solution)/shard_map/ppermute | solution.py:10
  128.6 31.1 %collective-permute-start.17 = (bf16[1,128,128]{2,1,0:T(8,128)(2,1)S(1)}, bf16[1,128,128]{2,1,0:T(8,128)(2,1)S(1)}, u32[]{:S(2)}, u32[]{:S(2)}) collective-permute-start(bf16[1,128,128]{2,1,0:T(8,128)(2,1)S(1)} %get-tuple-element.57), channel_id=1, source_target_pairs={{1,0},{2,1},{3,2},{4,3},{5,4},{6,5},{7,6},{8,7},{9,8},{10,9},{11,1... | collective-permute-start | bytes 98312 | tf_op jit(solution)/shard_map/ppermute | solution.py:10
  130.5 35.8 %collective-permute-start.18 = (bf16[1,128,128]{2,1,0:T(8,128)(2,1)S(1)}, bf16[1,128,128]{2,1,0:T(8,128)(2,1)S(1)}, u32[]{:S(2)}, u32[]{:S(2)}) collective-permute-start(bf16[1,128,128]{2,1,0:T(8,128)(2,1)S(1)} %get-tuple-element.57), channel_id=1, source_target_pairs={{0,2},{1,3},{2,4},{3,5},{4,6},{5,7},{6,8},{7,9},{8,10},{9,11},{10,... | collective-permute-start | bytes 98312 | tf_op jit(solution)/shard_map/ppermute | solution.py:10
  132.8 34.8 %collective-permute-start.19 = (bf16[1,128,128]{2,1,0:T(8,128)(2,1)S(1)}, bf16[1,128,128]{2,1,0:T(8,128)(2,1)S(1)}, u32[]{:S(2)}, u32[]{:S(2)}) collective-permute-start(bf16[1,128,128]{2,1,0:T(8,128)(2,1)S(1)} %get-tuple-element.57), channel_id=1, source_target_pairs={{2,0},{3,1},{4,2},{5,3},{6,4},{7,5},{8,6},{9,7},{10,8},{11,9},{12,... | collective-permute-start | bytes 98312 | tf_op jit(solution)/shard_map/ppermute | solution.py:10
  134.1 35.7 %collective-permute-start.20 = (bf16[1,128,128]{2,1,0:T(8,128)(2,1)S(1)}, bf16[1,128,128]{2,1,0:T(8,128)(2,1)S(1)}, u32[]{:S(2)}, u32[]{:S(2)}) collective-permute-start(bf16[1,128,128]{2,1,0:T(8,128)(2,1)S(1)} %get-tuple-element.57), channel_id=1, source_target_pairs={{0,3},{1,4},{2,5},{3,6},{4,7},{5,8},{6,9},{7,10},{8,11},{9,12},{10... | collective-permute-start | bytes 98312 | tf_op jit(solution)/shard_map/ppermute | solution.py:10
  158.4 13.7 %collective-permute-start.21 = (bf16[1,128,128]{2,1,0:T(8,128)(2,1)S(1)}, bf16[1,128,128]{2,1,0:T(8,128)(2,1)S(1)}, u32[]{:S(2)}, u32[]{:S(2)}) collective-permute-start(bf16[1,128,128]{2,1,0:T(8,128)(2,1)S(1)} %get-tuple-element.57), channel_id=1, source_target_pairs={{3,0},{4,1},{5,2},{6,3},{7,4},{8,5},{9,6},{10,7},{11,8},{12,9},{13... | collective-permute-start | bytes 98312 | tf_op jit(solution)/shard_map/ppermute | solution.py:10
  159.7 18.8 %collective-permute-start.22 = (bf16[1,128,128]{2,1,0:T(8,128)(2,1)S(1)}, bf16[1,128,128]{2,1,0:T(8,128)(2,1)S(1)}, u32[]{:S(2)}, u32[]{:S(2)}) collective-permute-start(bf16[1,128,128]{2,1,0:T(8,128)(2,1)S(1)} %get-tuple-element.57), channel_id=1, source_target_pairs={{0,4},{1,5},{2,6},{3,7},{4,8},{5,9},{6,10},{7,11},{8,12},{9,13},{1... | collective-permute-start | bytes 98312 | tf_op jit(solution)/shard_map/ppermute | solution.py:10
  166.3 13.5 %collective-permute-start.23 = (bf16[1,128,128]{2,1,0:T(8,128)(2,1)S(1)}, bf16[1,128,128]{2,1,0:T(8,128)(2,1)S(1)}, u32[]{:S(2)}, u32[]{:S(2)}) collective-permute-start(bf16[1,128,128]{2,1,0:T(8,128)(2,1)S(1)} %get-tuple-element.57), channel_id=1, source_target_pairs={{4,0},{5,1},{6,2},{7,3},{8,4},{9,5},{10,6},{11,7},{12,8},{13,9},{1... | collective-permute-start | bytes 98312 | tf_op jit(solution)/shard_map/ppermute | solution.py:10
  167.6 18.2 %collective-permute-start.8 = (bf16[1,128,128]{2,1,0:T(8,128)(2,1)S(1)}, bf16[1,128,128]{2,1,0:T(8,128)(2,1)S(1)}, u32[]{:S(2)}, u32[]{:S(2)}) collective-permute-start(bf16[1,128,128]{2,1,0:T(8,128)(2,1)S(1)} %get-tuple-element.59), channel_id=1, source_target_pairs={{0,1},{1,2},{2,3},{3,4},{4,5},{5,6},{6,7},{7,8},{8,9},{9,10},{10,1... | collective-permute-start | bytes 98312 | tf_op jit(solution)/shard_map/ppermute | solution.py:10
  169.8 17.3 %collective-permute-start.9 = (bf16[1,128,128]{2,1,0:T(8,128)(2,1)S(1)}, bf16[1,128,128]{2,1,0:T(8,128)(2,1)S(1)}, u32[]{:S(2)}, u32[]{:S(2)}) collective-permute-start(bf16[1,128,128]{2,1,0:T(8,128)(2,1)S(1)} %get-tuple-element.59), channel_id=1, source_target_pairs={{1,0},{2,1},{3,2},{4,3},{5,4},{6,5},{7,6},{8,7},{9,8},{10,9},{11,1... | collective-permute-start | bytes 98312 | tf_op jit(solution)/shard_map/ppermute | solution.py:10
  172.0 24.0 %collective-permute-start.10 = (bf16[1,128,128]{2,1,0:T(8,128)(2,1)S(1)}, bf16[1,128,128]{2,1,0:T(8,128)(2,1)S(1)}, u32[]{:S(2)}, u32[]{:S(2)}) collective-permute-start(bf16[1,128,128]{2,1,0:T(8,128)(2,1)S(1)} %get-tuple-element.59), channel_id=1, source_target_pairs={{0,2},{1,3},{2,4},{3,5},{4,6},{5,7},{6,8},{7,9},{8,10},{9,11},{10,... | collective-permute-start | bytes 98312 | tf_op jit(solution)/shard_map/ppermute | solution.py:10
  178.5 18.8 %collective-permute-start.11 = (bf16[1,128,128]{2,1,0:T(8,128)(2,1)S(1)}, bf16[1,128,128]{2,1,0:T(8,128)(2,1)S(1)}, u32[]{:S(2)}, u32[]{:S(2)}) collective-permute-start(bf16[1,128,128]{2,1,0:T(8,128)(2,1)S(1)} %get-tuple-element.59), channel_id=1, source_target_pairs={{2,0},{3,1},{4,2},{5,3},{6,4},{7,5},{8,6},{9,7},{10,8},{11,9},{12,... | collective-permute-start | bytes 98312 | tf_op jit(solution)/shard_map/ppermute | solution.py:10
  179.8 17.5 %collective-permute-start.12 = (bf16[1,128,128]{2,1,0:T(8,128)(2,1)S(1)}, bf16[1,128,128]{2,1,0:T(8,128)(2,1)S(1)}, u32[]{:S(2)}, u32[]{:S(2)}) collective-permute-start(bf16[1,128,128]{2,1,0:T(8,128)(2,1)S(1)} %get-tuple-element.59), channel_id=1, source_target_pairs={{0,3},{1,4},{2,5},{3,6},{4,7},{5,8},{6,9},{7,10},{8,11},{9,12},{10... | collective-permute-start | bytes 98312 | tf_op jit(solution)/shard_map/ppermute | solution.py:10
  185.9 11.5 %collective-permute-start.13 = (bf16[1,128,128]{2,1,0:T(8,128)(2,1)S(1)}, bf16[1,128,128]{2,1,0:T(8,128)(2,1)S(1)}, u32[]{:S(2)}, u32[]{:S(2)}) collective-permute-start(bf16[1,128,128]{2,1,0:T(8,128)(2,1)S(1)} %get-tuple-element.59), channel_id=1, source_target_pairs={{3,0},{4,1},{5,2},{6,3},{7,4},{8,5},{9,6},{10,7},{11,8},{12,9},{13... | collective-permute-start | bytes 98312 | tf_op jit(solution)/shard_map/ppermute | solution.py:10
  187.2 10.2 %collective-permute-start.14 = (bf16[1,128,128]{2,1,0:T(8,128)(2,1)S(1)}, bf16[1,128,128]{2,1,0:T(8,128)(2,1)S(1)}, u32[]{:S(2)}, u32[]{:S(2)}) collective-permute-start(bf16[1,128,128]{2,1,0:T(8,128)(2,1)S(1)} %get-tuple-element.59), channel_id=1, source_target_pairs={{0,4},{1,5},{2,6},{3,7},{4,8},{5,9},{6,10},{7,11},{8,12},{9,13},{1... | collective-permute-start | bytes 98312 | tf_op jit(solution)/shard_map/ppermute | solution.py:10
  196.0 6.0 %collective-permute-start.15 = (bf16[1,128,128]{2,1,0:T(8,128)(2,1)S(1)}, bf16[1,128,128]{2,1,0:T(8,128)(2,1)S(1)}, u32[]{:S(2)}, u32[]{:S(2)}) collective-permute-start(bf16[1,128,128]{2,1,0:T(8,128)(2,1)S(1)} %get-tuple-element.59), channel_id=1, source_target_pairs={{4,0},{5,1},{6,2},{7,3},{8,4},{9,5},{10,6},{11,7},{12,8},{13,9},{1... | collective-permute-start | bytes 98312 | tf_op jit(solution)/shard_map/ppermute | solution.py:10
Sparse Core Ops, SparseCore 0:
  46.8 74.6 all-gather.2
  125.1 112.6 all-gather.4
where the time goes:
time: 265 us; the launch traced here: 264 us
  waiting for transfers between devices  116 us (44%)
  starting transfers between devices  82.8 us (31%)
  local copies, waits for them, and re-layouts  25.5 us (10%)
  between operations  15.3 us (6%)
  matrix products  13.5 us (5%)
  other arithmetic  11.3 us (4%)
    ppermute x24, starting transfers between devices, passed_along(): return lax.ppermute(block, axis, route)  82.7 us
    all_gather x1, waiting for transfers between devices, on_device(): group_cells = lax.all_gather(cell_blocks, 'dp', axis=0, tiled=True)  73.8 us
    all_gather x1, waiting for transfers between devices, on_device(): panel_piece = lax.all_gather(panel, 'fsdp', axis=0, tiled=True)  34.5 us
    dot_general x1, matrix products, on_device(): jnp.einsum('tcka,ckab->tcb', picked, panel_piece, preferred_element_type=...  13.5 us
    gather x1, local copies, waits for them, and re-layouts, on_device(): picked = jnp.take(token_blocks, new_rows.reshape(-1), axis=1)  13.3 us
    unnamed x4, local copies, waits for them, and re-layouts  9.25 us
    ppermute x24, waiting for transfers between devices, passed_along(): return lax.ppermute(block, axis, route)  7.47 us
  transfers between devices with their start and end apart: 26, of which 4 were waited for; matrix products, arithmetic and copies ran while one was open for 10% of the time, Pallas kernels for 0%

commit v1 on v0

--- a/solution.py
+++ b/solution.py
@@ -2,6 +2,29 @@
 import jax.numpy as jnp
 from jax import lax
 from jax.sharding import PartitionSpec as P
+
+
+def supply_all_view(view, join_dim):
+    d_next = lax.psum(1, axis_name="fsdp")
+    high, n_now, tile_out = (d_next, lax.axis_index("fsdp"), view.shape[join_dim])
+    copies = tuple((dev * high if kk == join_dim else dev for kk, dev in enumerate(view.shape)))
+    step_out = jnp.zeros(copies, view.dtype)
+    x_now = lax.dynamic_update_slice_in_dim(step_out, view, n_now * tile_out, axis=join_dim)
+    arr_next = w_next = view
+    for pp in range(1, high // 2 + 1):
+        arr_next = lax.ppermute(
+            arr_next, axis_name="fsdp", perm=tuple(((kk, (kk + 1) % high) for kk in range(high)))
+        )
+        x_now = lax.dynamic_update_slice_in_dim(
+            x_now, arr_next, (n_now - pp) % high * tile_out, axis=join_dim
+        )
+        if 2 * pp < high:
+            taken_in = tuple(((kk, (kk - 1) % high) for kk in range(high)))
+            w_next = lax.ppermute(w_next, axis_name="fsdp", perm=taken_in)
+            x_now = lax.dynamic_update_slice_in_dim(
+                x_now, w_next, (n_now + pp) % high * tile_out, axis=join_dim
+            )
+    return x_now
 
 
 def passed_along(block, axis, distance):
@@ -67,7 +90,7 @@
     )
     token_count = tokens.shape[0]
     token_blocks = tokens.reshape(token_count, tokens.shape[1] // block_size, block_size)
-    panel_piece = lax.all_gather(panel, "fsdp", axis=0, tiled=True)
+    panel_piece = supply_all_view(panel, join_dim=0)
     count = panel_piece.shape[0]
     picked = jnp.take(token_blocks, new_rows.reshape(-1), axis=1)
     picked = picked.reshape(token_count, count, nonzero_count, block_size)

time: 265 us -> 388 us (1.46)
  starting transfers between devices: 82.8 us -> 148 us
  local copies, waits for them, and re-layouts: 25.5 us -> 53.7 us
  waiting for transfers between devices: 116 us -> 140 us
  other arithmetic: 11.3 us -> 16 us
    ppermute x0 -> x15, starting transfers between devices: none -> 64.3 us  [the longest x7 47.6 us: supply_all_view(): w_next = lax.ppermute(w_next, axis_name='fsdp', perm=taken_in)]
    ppermute x0 -> x15, waiting for transfers between devices: none -> 62.1 us  [the longest x8 34.8 us: supply_all_view(): lax.ppermute(arr_next, axis_name='fsdp', perm=tuple(((kk, (kk + 1) % high...]
    all_gather x1 -> x0, waiting for transfers between devices: 34.5 us -> none  [on_device(): panel_piece = lax.all_gather(panel, 'fsdp', axis=0, tiled=True)]
    dynamic_update_slice x0 -> x15, local copies, waits for them, and re-layouts: none -> 20.1 us  [the longest x8 10.7 us: supply_all_view(): lax.dynamic_update_slice_in_dim(x_now, arr_next, (n_now - pp) % high * ti...]
    broadcast_in_dim x0 -> x1, local copies, waits for them, and re-layouts: none -> 8.92 us  [supply_all_view(): step_out = jnp.zeros(copies, view.dtype)]
    unnamed x21, other arithmetic: 0.17 us -> 4.52 us
    unnamed x4 -> x18, local copies, waits for them, and re-layouts: 9.25 us -> 7.64 us
  transfers between devices with their start and end apart: 26 -> 40, of which waited for: 4 -> 9; matrix products, arithmetic and copies ran while one was open for 10% -> 12% of each run, Pallas kernels for 0% -> 0%
where the time goes in v1:
time: 388 us; the launch traced here: 386 us
  starting transfers between devices  148 us (38%)
  waiting for transfers between devices  140 us (36%)
  local copies, waits for them, and re-layouts  53.7 us (14%)
  other arithmetic  16 us (4%)
  between operations  15.5 us (4%)
  matrix products  13.4 us (3%)
    ppermute x24, starting transfers between devices, passed_along(): return lax.ppermute(block, axis, route)  83.4 us
    all_gather x1, waiting for transfers between devices, on_device(): group_cells = lax.all_gather(cell_blocks, 'dp', axis=0, tiled=True)  73.8 us
    ppermute x7, starting transfers between devices, supply_all_view(): w_next = lax.ppermute(w_next, axis_name='fsdp', perm=taken_in)  47.6 us
    ppermute x8, waiting for transfers between devices, supply_all_view(): lax.ppermute(arr_next, axis_name='fsdp', perm=tuple(((kk, (kk + 1) % high...  34.8 us
    ppermute x7, waiting for transfers between devices, supply_all_view(): w_next = lax.ppermute(w_next, axis_name='fsdp', perm=taken_in)  27.3 us
    ppermute x8, starting transfers between devices, supply_all_view(): lax.ppermute(arr_next, axis_name='fsdp', perm=tuple(((kk, (kk + 1) % high...  16.7 us
    dot_general x1, matrix products, on_device(): jnp.einsum('tcka,ckab->tcb', picked, panel_piece, preferred_element_type=...  13.4 us
    gather x1, local copies, waits for them, and re-layouts, on_device(): picked = jnp.take(token_blocks, new_rows.reshape(-1), axis=1)  13.4 us
  transfers between devices with their start and end apart: 40, of which 9 were waited for; matrix products, arithmetic and copies ran while one was open for 12% of the time, Pallas kernels for 0%

profile of v1, /device:TPU:1, one launch (start us, length us, event | category | flops | bytes accessed | tf_op | source)
XLA Modules:
  0.0 386.5 jit_solution(17579673034865341144)
XLA Ops:
  8.2 4.9 %collective-permute-start = (bf16[1,128,128]{2,1,0:T(8,128)(2,1)S(1)}, bf16[1,128,128]{2,1,0:T(8,128)(2,1)S(1)}, u32[]{:S(2)}, u32[]{:S(2)}) collective-permute-start(bf16[1,128,128]{2,1,0:T(8,128)(2,1)S(1)} %get-tuple-element.63), channel_id=1, source_target_pairs={{0,1},{1,2},{2,3},{3,4},{4,5},{5,6},{6,7},{7,8},{8,9},{9,10},{10,1... | collective-permute-start | bytes 98312 | tf_op jit(solution)/shard_map/ppermute | solution.py:33
  13.2 5.1 %collective-permute-start.1 = (bf16[1,128,128]{2,1,0:T(8,128)(2,1)S(1)}, bf16[1,128,128]{2,1,0:T(8,128)(2,1)S(1)}, u32[]{:S(2)}, u32[]{:S(2)}) collective-permute-start(bf16[1,128,128]{2,1,0:T(8,128)(2,1)S(1)} %get-tuple-element.63), channel_id=1, source_target_pairs={{1,0},{2,1},{3,2},{4,3},{5,4},{6,5},{7,6},{8,7},{9,8},{10,9},{11,1... | collective-permute-start | bytes 98312 | tf_op jit(solution)/shard_map/ppermute | solution.py:33
  18.3 1.3 collective-permute-start.2
  19.6 1.3 collective-permute-start.3
  20.9 5.0 %collective-permute-start.4 = (bf16[1,128,128]{2,1,0:T(8,128)(2,1)S(1)}, bf16[1,128,128]{2,1,0:T(8,128)(2,1)S(1)}, u32[]{:S(2)}, u32[]{:S(2)}) collective-permute-start(bf16[1,128,128]{2,1,0:T(8,128)(2,1)S(1)} %get-tuple-element.63), channel_id=1, source_target_pairs={{0,3},{1,4},{2,5},{3,6},{4,7},{5,8},{6,9},{7,10},{8,11},{9,12},{10... | collective-permute-start | bytes 98312 | tf_op jit(solution)/shard_map/ppermute | solution.py:33
  26.0 1.4 and_reduce_fusion
  27.3 1.3 select_reduce_fusion
  29.3 1.3 collective-permute-start.5
  30.6 9.2 %collective-permute-start.6 = (bf16[1,128,128]{2,1,0:T(8,128)(2,1)S(1)}, bf16[1,128,128]{2,1,0:T(8,128)(2,1)S(1)}, u32[]{:S(2)}, u32[]{:S(2)}) collective-permute-start(bf16[1,128,128]{2,1,0:T(8,128)(2,1)S(1)} %get-tuple-element.63), channel_id=1, source_target_pairs={{0,4},{1,5},{2,6},{3,7},{4,8},{5,9},{6,10},{7,11},{8,12},{9,13},{1... | collective-permute-start | bytes 98312 | tf_op jit(solution)/shard_map/ppermute | solution.py:33
  39.8 1.3 collective-permute-start.7
  41.3 4.1 %collective-permute-done.7 = bf16[1,128,128]{2,1,0:T(8,128)(2,1)S(1)} collective-permute-done((bf16[1,128,128]{2,1,0:T(8,128)(2,1)S(1)}, bf16[1,128,128]{2,1,0:T(8,128)(2,1)S(1)}, u32[]{:S(2)}, u32[]{:S(2)}) %collective-permute-start.7) | collective-permute-done | bytes 32800 | tf_op jit(solution)/shard_map/ppermute | solution.py:33
  45.4 1.3 fusion.8
  47.7 73.8 %all-gather.2.cloned.1.call-done = bf16[32,128,128]{2,1,0:T(8,128)(2,1)} async-done(((bf16[1,128,128]{2,1,0:T(8,128)(2,1)}), bf16[32,128,128]{2,1,0:T(8,128)(2,1)}) %all-gather.2.cloned.1.call-update) | async-done | bytes 1048592 | tf_op jit(solution)/shard_map/all_gather | solution.py:87
  121.4 1.9 gather_fusion
  124.0 8.9 %broadcast_in_dim.57 = bf16[112,4,128,128]{2,3,1,0:T(8,128)(2,1)} broadcast(bf16[]{:T(256)} %constant.154.clone.1), dimensions={} | broadcast | bytes 14680066 | tf_op jit(solution)/shard_map/broadcast_in_dim | solution.py:11
  133.0 1.2 constant_dynamic-update-slice_fusion.18
  134.2 3.1 collective-permute-start.8
  137.3 5.5 %collective-permute-start.9 = (bf16[7,4,128,128]{2,3,1,0:T(8,128)(2,1)S(1)}, bf16[7,4,128,128]{2,3,1,0:T(8,128)(2,1)}, u32[]{:S(2)}, u32[]{:S(2)}) collective-permute-start(bf16[7,4,128,128]{2,3,1,0:T(8,128)(2,1)S(1)} %get-tuple-element.54), channel_id=1, source_target_pairs={{0,480},{32,0},{64,32},{96,64},{128,96},{160,128},{192,160},{224,1... | collective-permute-start | bytes 2752520 | tf_op jit(solution)/shard_map/ppermute | solution.py:23
  142.8 18.3 %collective-permute-done.8 = bf16[7,4,128,128]{2,3,1,0:T(8,128)(2,1)S(1)} collective-permute-done((bf16[7,4,128,128]{2,3,1,0:T(8,128)(2,1)S(1)}, bf16[7,4,128,128]{2,3,1,0:T(8,128)(2,1)S(1)}, u32[]{:S(2)}, u32[]{:S(2)}) %collective-permute-start.8) | collective-permute-done | bytes 917536 | tf_op jit(solution)/shard_map/ppermute | solution.py:15
  161.1 1.9 collective-permute-start.10
  163.6 4.0 %collective-permute-start.31 = (bf16[1,128,128]{2,1,0:T(8,128)(2,1)S(1)}, bf16[1,128,128]{2,1,0:T(8,128)(2,1)S(1)}, u32[]{:S(2)}, u32[]{:S(2)}) collective-permute-start(bf16[1,128,128]{2,1,0:T(8,128)(2,1)S(1)} %get-tuple-element.59), channel_id=1, source_target_pairs={{0,1},{1,2},{2,3},{3,4},{4,5},{5,6},{6,7},{7,8},{8,9},{9,10},{10,1... | collective-permute-start | bytes 98312 | tf_op jit(solution)/shard_map/ppermute | solution.py:33
  167.7 1.9 collective-permute-start.32
  169.6 2.3 collective-permute-start.33
  172.1 7.0 %collective-permute-start.11 = (bf16[7,4,128,128]{2,3,1,0:T(8,128)(2,1)}, bf16[7,4,128,128]{2,3,1,0:T(8,128)(2,1)}, u32[]{:S(2)}, u32[]{:S(2)}) collective-permute-start(bf16[7,4,128,128]{2,3,1,0:T(8,128)(2,1)} %collective-permute-done.9), channel_id=1, source_target_pairs={{0,480},{32,0},{64,32},{96,64},{128,96},{160,128},{192,160},{224,1... | collective-permute-start | bytes 2752520 | tf_op jit(solution)/shard_map/ppermute | solution.py:23
  179.1 8.1 %collective-permute-done.10 = bf16[7,4,128,128]{2,3,1,0:T(8,128)(2,1)} collective-permute-done((bf16[7,4,128,128]{2,3,1,0:T(8,128)(2,1)S(1)}, bf16[7,4,128,128]{2,3,1,0:T(8,128)(2,1)}, u32[]{:S(2)}, u32[]{:S(2)}) %collective-permute-start.10) | collective-permute-done | bytes 917536 | tf_op jit(solution)/shard_map/ppermute | solution.py:15
  187.1 1.9 collective-permute-start.12
  191.3 13.4 %gather_fusion.1 = bf16[448,128,128]{2,1,0:T(8,128)(2,1)} fusion(bf16[128,32,128]{2,0,1:T(8,128)(2,1)S(1)} %copy.38, s32[1024]{0:T(1024)S(1)} %pad_clamp_fusion), kind=kCustom, calls=%fused_computation.1 | custom fusion | bytes 29361920 | tf_op jit(solution)/shard_map/jit(_take)/gather | solution.py:95
  204.7 1.3 collective-permute-start.34
  206.6 7.0 %collective-permute-start.35 = (bf16[1,128,128]{2,1,0:T(8,128)(2,1)S(1)}, bf16[1,128,128]{2,1,0:T(8,128)(2,1)S(1)}, u32[]{:S(2)}, u32[]{:S(2)}) collective-permute-start(bf16[1,128,128]{2,1,0:T(8,128)(2,1)S(1)} %get-tuple-element.59), channel_id=1, source_target_pairs={{0,3},{1,4},{2,5},{3,6},{4,7},{5,8},{6,9},{7,10},{8,11},{9,12},{10... | collective-permute-start | bytes 98312 | tf_op jit(solution)/shard_map/ppermute | solution.py:33
  214.2 1.3 collective-permute-start.36
  215.5 7.0 %collective-permute-start.13 = (bf16[7,4,128,128]{2,3,1,0:T(8,128)(2,1)}, bf16[7,4,128,128]{2,3,1,0:T(8,128)(2,1)S(1)}, u32[]{:S(2)}, u32[]{:S(2)}) collective-permute-start(bf16[7,4,128,128]{2,3,1,0:T(8,128)(2,1)} %collective-permute-done.11), channel_id=1, source_target_pairs={{0,480},{32,0},{64,32},{96,64},{128,96},{160,128},{192,160},{224,1... | collective-permute-start | bytes 2752520 | tf_op jit(solution)/shard_map/ppermute | solution.py:23
  222.5 1.9 collective-permute-start.14
  225.1 5.0 %collective-permute-start.37 = (bf16[1,128,128]{2,1,0:T(8,128)(2,1)S(1)}, bf16[1,128,128]{2,1,0:T(8,128)(2,1)S(1)}, u32[]{:S(2)}, u32[]{:S(2)}) collective-permute-start(bf16[1,128,128]{2,1,0:T(8,128)(2,1)S(1)} %get-tuple-element.59), channel_id=1, source_target_pairs={{0,4},{1,5},{2,6},{3,7},{4,8},{5,9},{6,10},{7,11},{8,12},{9,13},{1... | collective-permute-start | bytes 98312 | tf_op jit(solution)/shard_map/ppermute | solution.py:33
  230.7 1.3 collective-permute-start.38
  232.6 3.0 collective-permute-start.23
  236.2 1.9 collective-permute-start.24
  238.8 6.1 %collective-permute-start.25 = (bf16[1,128,128]{2,1,0:T(8,128)(2,1)S(1)}, bf16[1,128,128]{2,1,0:T(8,128)(2,1)S(1)}, u32[]{:S(2)}, u32[]{:S(2)}) collective-permute-start(bf16[1,128,128]{2,1,0:T(8,128)(2,1)S(1)} %get-tuple-element.61), channel_id=1, source_target_pairs={{0,2},{1,3},{2,4},{3,5},{4,6},{5,7},{6,8},{7,9},{8,10},{9,11},{10,... | collective-permute-start | bytes 98312 | tf_op jit(solution)/shard_map/ppermute | solution.py:33
  244.9 7.0 %collective-permute-start.15 = (bf16[7,4,128,128]{2,3,1,0:T(8,128)(2,1)S(1)}, bf16[7,4,128,128]{2,3,1,0:T(8,128)(2,1)S(1)}, u32[]{:S(2)}, u32[]{:S(2)}) collective-permute-start(bf16[7,4,128,128]{2,3,1,0:T(8,128)(2,1)S(1)} %collective-permute-done.13), channel_id=1, source_target_pairs={{0,480},{32,0},{64,32},{96,64},{128,96},{160,128},{192,160},{224,1... | collective-permute-start | bytes 2752520 | tf_op jit(solution)/shard_map/ppermute | solution.py:23
  251.9 1.9 collective-permute-start.16
  254.5 1.3 collective-permute-start.26
  255.8 6.3 %collective-permute-start.27 = (bf16[1,128,128]{2,1,0:T(8,128)(2,1)S(1)}, bf16[1,128,128]{2,1,0:T(8,128)(2,1)S(1)}, u32[]{:S(2)}, u32[]{:S(2)}) collective-permute-start(bf16[1,128,128]{2,1,0:T(8,128)(2,1)S(1)} %get-tuple-element.61), channel_id=1, source_target_pairs={{0,3},{1,4},{2,5},{3,6},{4,7},{5,8},{6,9},{7,10},{8,11},{9,12},{10... | collective-permute-start | bytes 98312 | tf_op jit(solution)/shard_map/ppermute | solution.py:33
  262.1 1.3 collective-permute-start.28
  263.4 8.8 %collective-permute-start.29 = (bf16[1,128,128]{2,1,0:T(8,128)(2,1)S(1)}, bf16[1,128,128]{2,1,0:T(8,128)(2,1)S(1)}, u32[]{:S(2)}, u32[]{:S(2)}) collective-permute-start(bf16[1,128,128]{2,1,0:T(8,128)(2,1)S(1)} %get-tuple-element.61), channel_id=1, source_target_pairs={{0,4},{1,5},{2,6},{3,7},{4,8},{5,9},{6,10},{7,11},{8,12},{9,13},{1... | collective-permute-start | bytes 98312 | tf_op jit(solution)/shard_map/ppermute | solution.py:33
  272.3 1.3 collective-permute-start.30
  273.6 7.0 %collective-permute-start.17 = (bf16[7,4,128,128]{2,3,1,0:T(8,128)(2,1)S(1)}, bf16[7,4,128,128]{2,3,1,0:T(8,128)(2,1)S(1)}, u32[]{:S(2)}, u32[]{:S(2)}) collective-permute-start(bf16[7,4,128,128]{2,3,1,0:T(8,128)(2,1)S(1)} %collective-permute-done.15), channel_id=1, source_target_pairs={{0,480},{32,0},{64,32},{96,64},{128,96},{160,128},{192,160},{224,1... | collective-permute-start | bytes 2752520 | tf_op jit(solution)/shard_map/ppermute | solution.py:23
  280.6 1.9 collective-permute-start.18
  282.5 2.1 dynamic-slice_select_fusion
  284.7 13.2 %collective-permute-done.17 = bf16[7,4,128,128]{2,3,1,0:T(8,128)(2,1)S(1)} collective-permute-done((bf16[7,4,128,128]{2,3,1,0:T(8,128)(2,1)S(1)}, bf16[7,4,128,128]{2,3,1,0:T(8,128)(2,1)S(1)}, u32[]{:S(2)}, u32[]{:S(2)}) %collective-permute-start.17) | collective-permute-done | bytes 917536 | tf_op jit(solution)/shard_map/ppermute | solution.py:23
  297.9 7.1 %collective-permute-start.19 = (bf16[7,4,128,128]{2,3,1,0:T(8,128)(2,1)S(1)}, bf16[7,4,128,128]{2,3,1,0:T(8,128)(2,1)S(1)}, u32[]{:S(2)}, u32[]{:S(2)}) collective-permute-start(bf16[7,4,128,128]{2,3,1,0:T(8,128)(2,1)S(1)} %collective-permute-done.17), channel_id=1, source_target_pairs={{0,480},{32,0},{64,32},{96,64},{128,96},{160,128},{192,160},{224,1... | collective-permute-start | bytes 2752520 | tf_op jit(solution)/shard_map/ppermute | solution.py:23
  305.0 1.3 dynamic-slice_select_fusion.1
  306.3 1.9 collective-permute-start.20
  308.2 1.1 constant_dynamic-update-slice_fusion.17
  309.3 2.2 constant_dynamic-update-slice_fusion.16
  311.5 2.2 constant_dynamic-update-slice_fusion.15
  313.7 2.2 constant_dynamic-update-slice_fusion.14
  316.0 2.2 constant_dynamic-update-slice_fusion.13
  319.2 4.3 %collective-permute-done.19 = bf16[7,4,128,128]{2,3,1,0:T(8,128)(2,1)S(1)} collective-permute-done((bf16[7,4,128,128]{2,3,1,0:T(8,128)(2,1)S(1)}, bf16[7,4,128,128]{2,3,1,0:T(8,128)(2,1)S(1)}, u32[]{:S(2)}, u32[]{:S(2)}) %collective-permute-start.19) | collective-permute-done | bytes 917536 | tf_op jit(solution)/shard_map/ppermute | solution.py:23
  323.5 7.1 %collective-permute-start.21 = (bf16[7,4,128,128]{2,3,1,0:T(8,128)(2,1)S(1)}, bf16[7,4,128,128]{2,3,1,0:T(8,128)(2,1)S(1)}, u32[]{:S(2)}, u32[]{:S(2)}) collective-permute-start(bf16[7,4,128,128]{2,3,1,0:T(8,128)(2,1)S(1)} %collective-permute-done.19), channel_id=1, source_target_pairs={{0,480},{32,0},{64,32},{96,64},{128,96},{160,128},{192,160},{224,1... | collective-permute-start | bytes 2752520 | tf_op jit(solution)/shard_map/ppermute | solution.py:23
  332.2 2.1 collective-permute-start.22
  337.3 1.1 constant_dynamic-update-slice_fusion.7
  340.4 9.8 %collective-permute-done.21 = bf16[7,4,128,128]{2,3,1,0:T(8,128)(2,1)S(1)} collective-permute-done((bf16[7,4,128,128]{2,3,1,0:T(8,128)(2,1)S(1)}, bf16[7,4,128,128]{2,3,1,0:T(8,128)(2,1)S(1)}, u32[]{:S(2)}, u32[]{:S(2)}) %collective-permute-start.21) | collective-permute-done | bytes 917536 | tf_op jit(solution)/shard_map/ppermute | solution.py:23
  351.2 7.9 %collective-permute-done.22 = bf16[7,4,128,128]{2,3,1,0:T(8,128)(2,1)S(1)} collective-permute-done((bf16[7,4,128,128]{2,3,1,0:T(8,128)(2,1)S(1)}, bf16[7,4,128,128]{2,3,1,0:T(8,128)(2,1)S(1)}, u32[]{:S(2)}, u32[]{:S(2)}) %collective-permute-start.22) | collective-permute-done | bytes 917536 | tf_op jit(solution)/shard_map/ppermute | solution.py:15
  360.1 13.4 %bitcast_convert_fusion = bf16[112,128,128]{2,1,0:T(8,128)(2,1)} fusion(bf16[112,4,128,128]{2,3,1,0:T(8,128)(2,1)} %constant_dynamic-update-slice_fusion.3, bf16[128,112,4,128]{3,0,2,1:T(8,128)(2,1)} %bitcast.15, pred[112,4]{1,0:T(8,128)(4,1)S(1)} %copy.35), kind=kOutput, calls=%fused_computation.5 | convolution fusion | flops 1888223232 | bytes 33030592 | tf_op jit(solution)/shard_map/tcka,ckab->tcb/dot_general | solution.py:97
  373.5 6.1 %copy.39 = bf16[128,14336]{1,0:T(8,128)(2,1)} copy(bf16[128,14336]{0,1:T(8,128)(2,1)} %bitcast.17) | data formatting | bytes 7340032
  (98 shorter events, 20.5 us)
Async XLA Ops:
  7.2 155.8 %copy-start.3 = (f32[1,128,128]{2,1,0:T(8,128)S(1)}, f32[1,128,128]{2,1,0:T(8,128)}, u32[]{:S(2)}) copy-start(f32[1,128,128]{2,1,0:T(8,128)} %param.11) | copy-start | bytes 196612
  7.2 164.7 %copy-start.6 = (s32[112,4]{0,1:T(4,128)S(1)}, s32[112,4]{0,1:T(4,128)}, u32[]{:S(2)}) copy-start(s32[112,4]{0,1:T(4,128)} %param.15) | copy-start | bytes 5380
  7.2 181.9 %copy-start.4 = (f32[1,128,128]{2,1,0:T(8,128)S(1)}, f32[1,128,128]{2,1,0:T(8,128)}, u32[]{:S(2)}) copy-start(f32[1,128,128]{2,1,0:T(8,128)} %param.10) | copy-start | bytes 196612
  7.2 182.5 %copy-start = (bf16[128,4096]{1,0:T(8,128)(2,1)S(1)}, bf16[128,4096]{1,0:T(8,128)(2,1)}, u32[]{:S(2)}) copy-start(bf16[128,4096]{1,0:T(8,128)(2,1)} %param.8) | copy-start | bytes 3145732
  7.2 114.2 %all-gather.2.cloned.1.call-start = ((), (), s32[]{:S(2)}) async-start(), calls=%async_computation | async-start | bytes 1081344 | tf_op jit(solution)/shard_map/all_gather | solution.py:87
  8.2 21.1 %collective-permute-start = (bf16[1,128,128]{2,1,0:T(8,128)(2,1)S(1)}, bf16[1,128,128]{2,1,0:T(8,128)(2,1)S(1)}, u32[]{:S(2)}, u32[]{:S(2)}) collective-permute-start(bf16[1,128,128]{2,1,0:T(8,128)(2,1)S(1)} %get-tuple-element.63), channel_id=1, source_target_pairs={{0,1},{1,2},{2,3},{3,4},{4,5},{5,6},{6,7},{7,8},{8,9},{9,10},{10,1... | collective-permute-start | bytes 98312 | tf_op jit(solution)/shard_map/ppermute | solution.py:33
  13.2 17.5 %collective-permute-start.1 = (bf16[1,128,128]{2,1,0:T(8,128)(2,1)S(1)}, bf16[1,128,128]{2,1,0:T(8,128)(2,1)S(1)}, u32[]{:S(2)}, u32[]{:S(2)}) collective-permute-start(bf16[1,128,128]{2,1,0:T(8,128)(2,1)S(1)} %get-tuple-element.63), channel_id=1, source_target_pairs={{1,0},{2,1},{3,2},{4,3},{5,4},{6,5},{7,6},{8,7},{9,8},{10,9},{11,1... | collective-permute-start | bytes 98312 | tf_op jit(solution)/shard_map/ppermute | solution.py:33
  18.3 21.5 %collective-permute-start.2 = (bf16[1,128,128]{2,1,0:T(8,128)(2,1)S(1)}, bf16[1,128,128]{2,1,0:T(8,128)(2,1)S(1)}, u32[]{:S(2)}, u32[]{:S(2)}) collective-permute-start(bf16[1,128,128]{2,1,0:T(8,128)(2,1)S(1)} %get-tuple-element.63), channel_id=1, source_target_pairs={{0,2},{1,3},{2,4},{3,5},{4,6},{5,7},{6,8},{7,9},{8,10},{9,11},{10,... | collective-permute-start | bytes 98312 | tf_op jit(solution)/shard_map/ppermute | solution.py:33
  19.6 21.5 %collective-permute-start.3 = (bf16[1,128,128]{2,1,0:T(8,128)(2,1)S(1)}, bf16[1,128,128]{2,1,0:T(8,128)(2,1)S(1)}, u32[]{:S(2)}, u32[]{:S(2)}) collective-permute-start(bf16[1,128,128]{2,1,0:T(8,128)(2,1)S(1)} %get-tuple-element.63), channel_id=1, source_target_pairs={{2,0},{3,1},{4,2},{5,3},{6,4},{7,5},{8,6},{9,7},{10,8},{11,9},{12,... | collective-permute-start | bytes 98312 | tf_op jit(solution)/shard_map/ppermute | solution.py:33
  20.9 20.3 %collective-permute-start.4 = (bf16[1,128,128]{2,1,0:T(8,128)(2,1)S(1)}, bf16[1,128,128]{2,1,0:T(8,128)(2,1)S(1)}, u32[]{:S(2)}, u32[]{:S(2)}) collective-permute-start(bf16[1,128,128]{2,1,0:T(8,128)(2,1)S(1)} %get-tuple-element.63), channel_id=1, source_target_pairs={{0,3},{1,4},{2,5},{3,6},{4,7},{5,8},{6,9},{7,10},{8,11},{9,12},{10... | collective-permute-start | bytes 98312 | tf_op jit(solution)/shard_map/ppermute | solution.py:33
  29.3 11.9 %collective-permute-start.5 = (bf16[1,128,128]{2,1,0:T(8,128)(2,1)S(1)}, bf16[1,128,128]{2,1,0:T(8,128)(2,1)S(1)}, u32[]{:S(2)}, u32[]{:S(2)}) collective-permute-start(bf16[1,128,128]{2,1,0:T(8,128)(2,1)S(1)} %get-tuple-element.63), channel_id=1, source_target_pairs={{3,0},{4,1},{5,2},{6,3},{7,4},{8,5},{9,6},{10,7},{11,8},{12,9},{13... | collective-permute-start | bytes 98312 | tf_op jit(solution)/shard_map/ppermute | solution.py:33
  30.6 10.6 %collective-permute-start.6 = (bf16[1,128,128]{2,1,0:T(8,128)(2,1)S(1)}, bf16[1,128,128]{2,1,0:T(8,128)(2,1)S(1)}, u32[]{:S(2)}, u32[]{:S(2)}) collective-permute-start(bf16[1,128,128]{2,1,0:T(8,128)(2,1)S(1)} %get-tuple-element.63), channel_id=1, source_target_pairs={{0,4},{1,5},{2,6},{3,7},{4,8},{5,9},{6,10},{7,11},{8,12},{9,13},{1... | collective-permute-start | bytes 98312 | tf_op jit(solution)/shard_map/ppermute | solution.py:33
  39.8 5.6 %collective-permute-start.7 = (bf16[1,128,128]{2,1,0:T(8,128)(2,1)S(1)}, bf16[1,128,128]{2,1,0:T(8,128)(2,1)S(1)}, u32[]{:S(2)}, u32[]{:S(2)}) collective-permute-start(bf16[1,128,128]{2,1,0:T(8,128)(2,1)S(1)} %get-tuple-element.63), channel_id=1, source_target_pairs={{4,0},{5,1},{6,2},{7,3},{8,4},{9,5},{10,6},{11,7},{12,8},{13,9},{1... | collective-permute-start | bytes 98312 | tf_op jit(solution)/shard_map/ppermute | solution.py:33
  134.2 26.9 %collective-permute-start.8 = (bf16[7,4,128,128]{2,3,1,0:T(8,128)(2,1)S(1)}, bf16[7,4,128,128]{2,3,1,0:T(8,128)(2,1)S(1)}, u32[]{:S(2)}, u32[]{:S(2)}) collective-permute-start(bf16[7,4,128,128]{2,3,1,0:T(8,128)(2,1)S(1)} %get-tuple-element.54), channel_id=1, source_target_pairs={{0,32},{32,64},{64,96},{96,128},{128,160},{160,192},{192,224},{224... | collective-permute-start | bytes 2752520 | tf_op jit(solution)/shard_map/ppermute | solution.py:15
  137.3 34.8 %collective-permute-start.9 = (bf16[7,4,128,128]{2,3,1,0:T(8,128)(2,1)S(1)}, bf16[7,4,128,128]{2,3,1,0:T(8,128)(2,1)}, u32[]{:S(2)}, u32[]{:S(2)}) collective-permute-start(bf16[7,4,128,128]{2,3,1,0:T(8,128)(2,1)S(1)} %get-tuple-element.54), channel_id=1, source_target_pairs={{0,480},{32,0},{64,32},{96,64},{128,96},{160,128},{192,160},{224,1... | collective-permute-start | bytes 2752520 | tf_op jit(solution)/shard_map/ppermute | solution.py:23
  161.1 29.3 %copy-start.1 = (bf16[7,4,128,128]{2,3,1,0:T(8,128)(2,1)}, bf16[7,4,128,128]{2,3,1,0:T(8,128)(2,1)S(1)}, u32[]{:S(2)}) copy-start(bf16[7,4,128,128]{2,3,1,0:T(8,128)(2,1)S(1)} %collective-permute-done.8) | copy-start | bytes 2752516
  161.1 26.1 %collective-permute-start.10 = (bf16[7,4,128,128]{2,3,1,0:T(8,128)(2,1)S(1)}, bf16[7,4,128,128]{2,3,1,0:T(8,128)(2,1)}, u32[]{:S(2)}, u32[]{:S(2)}) collective-permute-start(bf16[7,4,128,128]{2,3,1,0:T(8,128)(2,1)S(1)} %collective-permute-done.8), channel_id=1, source_target_pairs={{0,32},{32,64},{64,96},{96,128},{128,160},{160,192},{192,224},{224... | collective-permute-start | bytes 2752520 | tf_op jit(solution)/shard_map/ppermute | solution.py:15
  163.6 41.0 %collective-permute-start.31 = (bf16[1,128,128]{2,1,0:T(8,128)(2,1)S(1)}, bf16[1,128,128]{2,1,0:T(8,128)(2,1)S(1)}, u32[]{:S(2)}, u32[]{:S(2)}) collective-permute-start(bf16[1,128,128]{2,1,0:T(8,128)(2,1)S(1)} %get-tuple-element.59), channel_id=1, source_target_pairs={{0,1},{1,2},{2,3},{3,4},{4,5},{5,6},{6,7},{7,8},{8,9},{9,10},{10,1... | collective-permute-start | bytes 98312 | tf_op jit(solution)/shard_map/ppermute | solution.py:33
  167.7 39.0 %collective-permute-start.32 = (bf16[1,128,128]{2,1,0:T(8,128)(2,1)S(1)}, bf16[1,128,128]{2,1,0:T(8,128)(2,1)S(1)}, u32[]{:S(2)}, u32[]{:S(2)}) collective-permute-start(bf16[1,128,128]{2,1,0:T(8,128)(2,1)S(1)} %get-tuple-element.59), channel_id=1, source_target_pairs={{1,0},{2,1},{3,2},{4,3},{5,4},{6,5},{7,6},{8,7},{9,8},{10,9},{11,1... | collective-permute-start | bytes 98312 | tf_op jit(solution)/shard_map/ppermute | solution.py:33
  169.6 44.7 %collective-permute-start.33 = (bf16[1,128,128]{2,1,0:T(8,128)(2,1)S(1)}, bf16[1,128,128]{2,1,0:T(8,128)(2,1)S(1)}, u32[]{:S(2)}, u32[]{:S(2)}) collective-permute-start(bf16[1,128,128]{2,1,0:T(8,128)(2,1)S(1)} %get-tuple-element.59), channel_id=1, source_target_pairs={{0,2},{1,3},{2,4},{3,5},{4,6},{5,7},{6,8},{7,9},{8,10},{9,11},{10,... | collective-permute-start | bytes 98312 | tf_op jit(solution)/shard_map/ppermute | solution.py:33
  172.1 43.4 %collective-permute-start.11 = (bf16[7,4,128,128]{2,3,1,0:T(8,128)(2,1)}, bf16[7,4,128,128]{2,3,1,0:T(8,128)(2,1)}, u32[]{:S(2)}, u32[]{:S(2)}) collective-permute-start(bf16[7,4,128,128]{2,3,1,0:T(8,128)(2,1)} %collective-permute-done.9), channel_id=1, source_target_pairs={{0,480},{32,0},{64,32},{96,64},{128,96},{160,128},{192,160},{224,1... | collective-permute-start | bytes 2752520 | tf_op jit(solution)/shard_map/ppermute | solution.py:23
  187.1 35.4 %collective-permute-start.12 = (bf16[7,4,128,128]{2,3,1,0:T(8,128)(2,1)}, bf16[7,4,128,128]{2,3,1,0:T(8,128)(2,1)}, u32[]{:S(2)}, u32[]{:S(2)}) collective-permute-start(bf16[7,4,128,128]{2,3,1,0:T(8,128)(2,1)} %collective-permute-done.10), channel_id=1, source_target_pairs={{0,32},{32,64},{64,96},{96,128},{128,160},{160,192},{192,224},{224... | collective-permute-start | bytes 2752520 | tf_op jit(solution)/shard_map/ppermute | solution.py:15
  191.3 64.5 %copy-start.5 = (f32[9,128,128]{2,1,0:T(8,128)S(1)}, f32[9,128,128]{2,1,0:T(8,128)}, u32[]{:S(2)}) copy-start(f32[9,128,128]{2,1,0:T(8,128)} %get-tuple-element.62) | copy-start | bytes 1769476
  191.3 116.9 %copy-start.2 = (bf16[7,4,128,128]{2,3,1,0:T(8,128)(2,1)S(1)}, bf16[7,4,128,128]{2,3,1,0:T(8,128)(2,1)}, u32[]{:S(2)}) copy-start(bf16[7,4,128,128]{2,3,1,0:T(8,128)(2,1)} %copy-done.1) | copy-start | bytes 2752516
  204.7 20.4 %collective-permute-start.34 = (bf16[1,128,128]{2,1,0:T(8,128)(2,1)S(1)}, bf16[1,128,128]{2,1,0:T(8,128)(2,1)S(1)}, u32[]{:S(2)}, u32[]{:S(2)}) collective-permute-start(bf16[1,128,128]{2,1,0:T(8,128)(2,1)S(1)} %get-tuple-element.59), channel_id=1, source_target_pairs={{2,0},{3,1},{4,2},{5,3},{6,4},{7,5},{8,6},{9,7},{10,8},{11,9},{12,... | collective-permute-start | bytes 98312 | tf_op jit(solution)/shard_map/ppermute | solution.py:33
  206.6 24.1 %collective-permute-start.35 = (bf16[1,128,128]{2,1,0:T(8,128)(2,1)S(1)}, bf16[1,128,128]{2,1,0:T(8,128)(2,1)S(1)}, u32[]{:S(2)}, u32[]{:S(2)}) collective-permute-start(bf16[1,128,128]{2,1,0:T(8,128)(2,1)S(1)} %get-tuple-element.59), channel_id=1, source_target_pairs={{0,3},{1,4},{2,5},{3,6},{4,7},{5,8},{6,9},{7,10},{8,11},{9,12},{10... | collective-permute-start | bytes 98312 | tf_op jit(solution)/shard_map/ppermute | solution.py:33
  214.2 18.4 %collective-permute-start.36 = (bf16[1,128,128]{2,1,0:T(8,128)(2,1)S(1)}, bf16[1,128,128]{2,1,0:T(8,128)(2,1)S(1)}, u32[]{:S(2)}, u32[]{:S(2)}) collective-permute-start(bf16[1,128,128]{2,1,0:T(8,128)(2,1)S(1)} %get-tuple-element.59), channel_id=1, source_target_pairs={{3,0},{4,1},{5,2},{6,3},{7,4},{8,5},{9,6},{10,7},{11,8},{12,9},{13... | collective-permute-start | bytes 98312 | tf_op jit(solution)/shard_map/ppermute | solution.py:33
  215.5 29.4 %collective-permute-start.13 = (bf16[7,4,128,128]{2,3,1,0:T(8,128)(2,1)}, bf16[7,4,128,128]{2,3,1,0:T(8,128)(2,1)S(1)}, u32[]{:S(2)}, u32[]{:S(2)}) collective-permute-start(bf16[7,4,128,128]{2,3,1,0:T(8,128)(2,1)} %collective-permute-done.11), channel_id=1, source_target_pairs={{0,480},{32,0},{64,32},{96,64},{128,96},{160,128},{192,160},{224,1... | collective-permute-start | bytes 2752520 | tf_op jit(solution)/shard_map/ppermute | solution.py:23
  222.5 29.4 %collective-permute-start.14 = (bf16[7,4,128,128]{2,3,1,0:T(8,128)(2,1)}, bf16[7,4,128,128]{2,3,1,0:T(8,128)(2,1)S(1)}, u32[]{:S(2)}, u32[]{:S(2)}) collective-permute-start(bf16[7,4,128,128]{2,3,1,0:T(8,128)(2,1)} %collective-permute-done.12), channel_id=1, source_target_pairs={{0,32},{32,64},{64,96},{96,128},{128,160},{160,192},{192,224},{224... | collective-permute-start | bytes 2752520 | tf_op jit(solution)/shard_map/ppermute | solution.py:15
  225.1 11.2 %collective-permute-start.37 = (bf16[1,128,128]{2,1,0:T(8,128)(2,1)S(1)}, bf16[1,128,128]{2,1,0:T(8,128)(2,1)S(1)}, u32[]{:S(2)}, u32[]{:S(2)}) collective-permute-start(bf16[1,128,128]{2,1,0:T(8,128)(2,1)S(1)} %get-tuple-element.59), channel_id=1, source_target_pairs={{0,4},{1,5},{2,6},{3,7},{4,8},{5,9},{6,10},{7,11},{8,12},{9,13},{1... | collective-permute-start | bytes 98312 | tf_op jit(solution)/shard_map/ppermute | solution.py:33
  230.7 8.1 %collective-permute-start.38 = (bf16[1,128,128]{2,1,0:T(8,128)(2,1)S(1)}, bf16[1,128,128]{2,1,0:T(8,128)(2,1)S(1)}, u32[]{:S(2)}, u32[]{:S(2)}) collective-permute-start(bf16[1,128,128]{2,1,0:T(8,128)(2,1)S(1)} %get-tuple-element.59), channel_id=1, source_target_pairs={{4,0},{5,1},{6,2},{7,3},{8,4},{9,5},{10,6},{11,7},{12,8},{13,9},{1... | collective-permute-start | bytes 98312 | tf_op jit(solution)/shard_map/ppermute | solution.py:33
  232.6 21.9 %collective-permute-start.23 = (bf16[1,128,128]{2,1,0:T(8,128)(2,1)S(1)}, bf16[1,128,128]{2,1,0:T(8,128)(2,1)S(1)}, u32[]{:S(2)}, u32[]{:S(2)}) collective-permute-start(bf16[1,128,128]{2,1,0:T(8,128)(2,1)S(1)} %get-tuple-element.61), channel_id=1, source_target_pairs={{0,1},{1,2},{2,3},{3,4},{4,5},{5,6},{6,7},{7,8},{8,9},{9,10},{10,1... | collective-permute-start | bytes 98312 | tf_op jit(solution)/shard_map/ppermute | solution.py:33
  236.2 19.5 %collective-permute-start.24 = (bf16[1,128,128]{2,1,0:T(8,128)(2,1)S(1)}, bf16[1,128,128]{2,1,0:T(8,128)(2,1)S(1)}, u32[]{:S(2)}, u32[]{:S(2)}) collective-permute-start(bf16[1,128,128]{2,1,0:T(8,128)(2,1)S(1)} %get-tuple-element.61), channel_id=1, source_target_pairs={{1,0},{2,1},{3,2},{4,3},{5,4},{6,5},{7,6},{8,7},{9,8},{10,9},{11,1... | collective-permute-start | bytes 98312 | tf_op jit(solution)/shard_map/ppermute | solution.py:33
  238.8 23.3 %collective-permute-start.25 = (bf16[1,128,128]{2,1,0:T(8,128)(2,1)S(1)}, bf16[1,128,128]{2,1,0:T(8,128)(2,1)S(1)}, u32[]{:S(2)}, u32[]{:S(2)}) collective-permute-start(bf16[1,128,128]{2,1,0:T(8,128)(2,1)S(1)} %get-tuple-element.61), channel_id=1, source_target_pairs={{0,2},{1,3},{2,4},{3,5},{4,6},{5,7},{6,8},{7,9},{8,10},{9,11},{10,... | collective-permute-start | bytes 98312 | tf_op jit(solution)/shard_map/ppermute | solution.py:33
  244.9 28.6 %collective-permute-start.15 = (bf16[7,4,128,128]{2,3,1,0:T(8,128)(2,1)S(1)}, bf16[7,4,128,128]{2,3,1,0:T(8,128)(2,1)S(1)}, u32[]{:S(2)}, u32[]{:S(2)}) collective-permute-start(bf16[7,4,128,128]{2,3,1,0:T(8,128)(2,1)S(1)} %collective-permute-done.13), channel_id=1, source_target_pairs={{0,480},{32,0},{64,32},{96,64},{128,96},{160,128},{192,160},{224,1... | collective-permute-start | bytes 2752520 | tf_op jit(solution)/shard_map/ppermute | solution.py:23
  251.9 28.6 %collective-permute-start.16 = (bf16[7,4,128,128]{2,3,1,0:T(8,128)(2,1)S(1)}, bf16[7,4,128,128]{2,3,1,0:T(8,128)(2,1)S(1)}, u32[]{:S(2)}, u32[]{:S(2)}) collective-permute-start(bf16[7,4,128,128]{2,3,1,0:T(8,128)(2,1)S(1)} %collective-permute-done.14), channel_id=1, source_target_pairs={{0,32},{32,64},{64,96},{96,128},{128,160},{160,192},{192,224},{224... | collective-permute-start | bytes 2752520 | tf_op jit(solution)/shard_map/ppermute | solution.py:15
  254.5 9.0 %collective-permute-start.26 = (bf16[1,128,128]{2,1,0:T(8,128)(2,1)S(1)}, bf16[1,128,128]{2,1,0:T(8,128)(2,1)S(1)}, u32[]{:S(2)}, u32[]{:S(2)}) collective-permute-start(bf16[1,128,128]{2,1,0:T(8,128)(2,1)S(1)} %get-tuple-element.61), channel_id=1, source_target_pairs={{2,0},{3,1},{4,2},{5,3},{6,4},{7,5},{8,6},{9,7},{10,8},{11,9},{12,... | collective-permute-start | bytes 98312 | tf_op jit(solution)/shard_map/ppermute | solution.py:33
  255.8 16.5 %collective-permute-start.27 = (bf16[1,128,128]{2,1,0:T(8,128)(2,1)S(1)}, bf16[1,128,128]{2,1,0:T(8,128)(2,1)S(1)}, u32[]{:S(2)}, u32[]{:S(2)}) collective-permute-start(bf16[1,128,128]{2,1,0:T(8,128)(2,1)S(1)} %get-tuple-element.61), channel_id=1, source_target_pairs={{0,3},{1,4},{2,5},{3,6},{4,7},{5,8},{6,9},{7,10},{8,11},{9,12},{10... | collective-permute-start | bytes 98312 | tf_op jit(solution)/shard_map/ppermute | solution.py:33
  262.1 20.4 %collective-permute-start.28 = (bf16[1,128,128]{2,1,0:T(8,128)(2,1)S(1)}, bf16[1,128,128]{2,1,0:T(8,128)(2,1)S(1)}, u32[]{:S(2)}, u32[]{:S(2)}) collective-permute-start(bf16[1,128,128]{2,1,0:T(8,128)(2,1)S(1)} %get-tuple-element.61), channel_id=1, source_target_pairs={{3,0},{4,1},{5,2},{6,3},{7,4},{8,5},{9,6},{10,7},{11,8},{12,9},{13... | collective-permute-start | bytes 98312 | tf_op jit(solution)/shard_map/ppermute | solution.py:33
  263.4 19.1 %collective-permute-start.29 = (bf16[1,128,128]{2,1,0:T(8,128)(2,1)S(1)}, bf16[1,128,128]{2,1,0:T(8,128)(2,1)S(1)}, u32[]{:S(2)}, u32[]{:S(2)}) collective-permute-start(bf16[1,128,128]{2,1,0:T(8,128)(2,1)S(1)} %get-tuple-element.61), channel_id=1, source_target_pairs={{0,4},{1,5},{2,6},{3,7},{4,8},{5,9},{6,10},{7,11},{8,12},{9,13},{1... | collective-permute-start | bytes 98312 | tf_op jit(solution)/shard_map/ppermute | solution.py:33
  272.3 12.4 %collective-permute-start.30 = (bf16[1,128,128]{2,1,0:T(8,128)(2,1)S(1)}, bf16[1,128,128]{2,1,0:T(8,128)(2,1)S(1)}, u32[]{:S(2)}, u32[]{:S(2)}) collective-permute-start(bf16[1,128,128]{2,1,0:T(8,128)(2,1)S(1)} %get-tuple-element.61), channel_id=1, source_target_pairs={{4,0},{5,1},{6,2},{7,3},{8,4},{9,5},{10,6},{11,7},{12,8},{13,9},{1... | collective-permute-start | bytes 98312 | tf_op jit(solution)/shard_map/ppermute | solution.py:33
  273.6 24.3 %collective-permute-start.17 = (bf16[7,4,128,128]{2,3,1,0:T(8,128)(2,1)S(1)}, bf16[7,4,128,128]{2,3,1,0:T(8,128)(2,1)S(1)}, u32[]{:S(2)}, u32[]{:S(2)}) collective-permute-start(bf16[7,4,128,128]{2,3,1,0:T(8,128)(2,1)S(1)} %collective-permute-done.15), channel_id=1, source_target_pairs={{0,480},{32,0},{64,32},{96,64},{128,96},{160,128},{192,160},{224,1... | collective-permute-start | bytes 2752520 | tf_op jit(solution)/shard_map/ppermute | solution.py:23
  280.6 25.8 %collective-permute-start.18 = (bf16[7,4,128,128]{2,3,1,0:T(8,128)(2,1)S(1)}, bf16[7,4,128,128]{2,3,1,0:T(8,128)(2,1)S(1)}, u32[]{:S(2)}, u32[]{:S(2)}) collective-permute-start(bf16[7,4,128,128]{2,3,1,0:T(8,128)(2,1)S(1)} %collective-permute-done.16), channel_id=1, source_target_pairs={{0,32},{32,64},{64,96},{96,128},{128,160},{160,192},{192,224},{224... | collective-permute-start | bytes 2752520 | tf_op jit(solution)/shard_map/ppermute | solution.py:15
  297.9 25.6 %collective-permute-start.19 = (bf16[7,4,128,128]{2,3,1,0:T(8,128)(2,1)S(1)}, bf16[7,4,128,128]{2,3,1,0:T(8,128)(2,1)S(1)}, u32[]{:S(2)}, u32[]{:S(2)}) collective-permute-start(bf16[7,4,128,128]{2,3,1,0:T(8,128)(2,1)S(1)} %collective-permute-done.17), channel_id=1, source_target_pairs={{0,480},{32,0},{64,32},{96,64},{128,96},{160,128},{192,160},{224,1... | collective-permute-start | bytes 2752520 | tf_op jit(solution)/shard_map/ppermute | solution.py:23
  306.3 25.9 %collective-permute-start.20 = (bf16[7,4,128,128]{2,3,1,0:T(8,128)(2,1)S(1)}, bf16[7,4,128,128]{2,3,1,0:T(8,128)(2,1)S(1)}, u32[]{:S(2)}, u32[]{:S(2)}) collective-permute-start(bf16[7,4,128,128]{2,3,1,0:T(8,128)(2,1)S(1)} %collective-permute-done.18), channel_id=1, source_target_pairs={{0,32},{32,64},{64,96},{96,128},{128,160},{160,192},{192,224},{224... | collective-permute-start | bytes 2752520 | tf_op jit(solution)/shard_map/ppermute | solution.py:15
  323.5 26.7 %collective-permute-start.21 = (bf16[7,4,128,128]{2,3,1,0:T(8,128)(2,1)S(1)}, bf16[7,4,128,128]{2,3,1,0:T(8,128)(2,1)S(1)}, u32[]{:S(2)}, u32[]{:S(2)}) collective-permute-start(bf16[7,4,128,128]{2,3,1,0:T(8,128)(2,1)S(1)} %collective-permute-done.19), channel_id=1, source_target_pairs={{0,480},{32,0},{64,32},{96,64},{128,96},{160,128},{192,160},{224,1... | collective-permute-start | bytes 2752520 | tf_op jit(solution)/shard_map/ppermute | solution.py:23
  332.2 27.0 %collective-permute-start.22 = (bf16[7,4,128,128]{2,3,1,0:T(8,128)(2,1)S(1)}, bf16[7,4,128,128]{2,3,1,0:T(8,128)(2,1)S(1)}, u32[]{:S(2)}, u32[]{:S(2)}) collective-permute-start(bf16[7,4,128,128]{2,3,1,0:T(8,128)(2,1)S(1)} %collective-permute-done.20), channel_id=1, source_target_pairs={{0,32},{32,64},{64,96},{96,128},{128,160},{160,192},{192,224},{224... | collective-permute-start | bytes 2752520 | tf_op jit(solution)/shard_map/ppermute | solution.py:15
Sparse Core Ops, SparseCore 0:
  46.8 74.5 all-gather.1
